TPU v7x, 512 devices: a whole 4x4x16 slice. The times are simulated.
512 devices in a mesh: prow: 16 (over y_hi, x, core), pcol: 32 (over y_lo, z).
Axes of the slice: x: 4, y: 4 (y_hi: 2, y_lo: 2; y = y_hi * 2 + y_lo), z: 16, core: 2. Of those that a mesh axis runs over, the one named last changes fastest.
Arguments:
- sep_inverse: bfloat16 [2, 16, 256, 1, 32, 256], P(None, 'prow', None, None, 'pcol'), may hold values from -2 to 30, as said below
- panels: bfloat16 [4, 2, 16, 256, 256], P(None, None, 'prow', 'pcol'), may hold values from -0.0625 to 0.0625
- ancestors: int32 [4, 32], replicated, may hold values from 0 to 1, as said below
- window_factor: bfloat16 [6, 256, 256], replicated, may hold values from -0.1875 to 0.1875
- diag_inverse: bfloat16 [4, 256, 256], replicated, may hold values from -1 to 4, as said below
Outputs:
- ys: float32 [4, 2, 16, 256, 256], P(None, None, 'prow', 'pcol')
- window_inverse: float32 [1024, 1024], P('prow', 'pcol')
Inputs may be any that keep to these rules, and one draw needn't show every extreme that they name: sep_inverse read as in the first step is symmetric. `diag_inverse`: each block is symmetric. ancestors[k + 1, t] <= ancestors[k, t]: a supernode's ancestor tiles lie among those of the one before it.
All inputs are finite; a program needn't handle non-finite values.
Results may differ from a plain program's by a relative error of at most 0.00035.
Values may be sent and summed in bfloat16 or wider, within the bound.
A program may use at most 64 MiB of HBM per device.

v0:
```python
import jax
import jax.numpy as jnp
from jax import lax
from jax.sharding import PartitionSpec as P


def broadcast(block, axis, owner):
    block = jnp.where(lax.axis_index(axis) == owner, block, jnp.zeros_like(block))
    return lax.psum(block, axis)


def product(operand_left, operand_right):
    return jnp.dot(
        operand_left,
        operand_right,
        precision=lax.Precision.HIGHEST,
        preferred_element_type=jnp.float32,
    )


def pair_index(earlier, later):
    return later * (later - 1) // 2 + earlier


def window_step(later, window_sums, window_factor, diag_inverse, window_blocks):
    coupled = []
    for earlier in range(later):
        running = window_sums[earlier]
        for partner in range(later):
            running = running + product(
                window_blocks[earlier, partner],
                window_factor[pair_index(partner, later)].astype(jnp.float32),
            )
        upper_block = -running
        window_blocks[earlier, later] = upper_block
        window_blocks[later, earlier] = upper_block.T
        coupled.append(upper_block)
    running = window_sums[later]
    for earlier in range(later):
        running = running + product(
            window_factor[pair_index(earlier, later)].astype(jnp.float32).T, coupled[earlier]
        )
    window_blocks[later, later] = diag_inverse[later].astype(jnp.float32) - running


def assemble_window(window_blocks, supernodes):
    return jnp.block(
        [
            [window_blocks[first, second] for second in range(supernodes)]
            for first in range(supernodes)
        ]
    )


def per_device(sep_inverse, panels, ancestors, window_factor, diag_inverse):
    prow_count = lax.axis_size("prow")
    pcol_count = lax.axis_size("pcol")
    row_index = lax.axis_index("prow")
    column_index = lax.axis_index("pcol")
    tile_rows = sep_inverse.shape[0]
    width = sep_inverse.shape[2]
    owned_count = sep_inverse.shape[3]
    supernodes = panels.shape[0]
    slice_rows = panels.shape[3]
    group_ratio = pcol_count // prow_count
    local_sep = sep_inverse.reshape(tile_rows, width, owned_count, width)
    window_blocks = {}
    columns = []
    for later in range(supernodes):
        tile_flags = lax.dynamic_slice_in_dim(
            ancestors[later].reshape(tile_rows, prow_count), row_index, 1, 1
        )
        keep_tiles = tile_flags.astype(jnp.bfloat16).reshape(tile_rows, 1, 1)
        own_piece = panels[later, :, 0] * keep_tiles
        full_rows = lax.all_gather(own_piece, "pcol", axis=1, tiled=True)
        grouped = full_rows.reshape(owned_count, group_ratio, width, width)
        picked = lax.dynamic_slice_in_dim(grouped, column_index // prow_count, 1, 1)[:, 0]
        owned_tiles = broadcast(picked, "prow", column_index % prow_count)

        def row_term(first_row, row_count, owned_tiles=owned_tiles):
            return jnp.einsum(
                "rbcd,cde->bre", local_sep, owned_tiles, preferred_element_type=jnp.float32
            )

        summed = lax.psum_scatter(
            row_term(jnp.int32(0), slice_rows * lax.axis_size("pcol")),
            "pcol",
            scatter_dimension=0,
            tiled=True,
        )
        row_total = jnp.transpose(summed, (1, 0, 2)).reshape(tile_rows * slice_rows, width)
        row_keep = jnp.repeat(
            tile_flags[:, 0].astype(jnp.float32),
            slice_rows,
            total_repeat_length=tile_rows * slice_rows,
        )
        carried = -row_total
        for earlier in range(later):
            carried = carried - product(
                columns[earlier], window_factor[pair_index(earlier, later)].astype(jnp.float32)
            )
        current = carried * row_keep[:, None]
        factor_rows = own_piece.reshape(tile_rows * slice_rows, width).astype(jnp.float32)
        window_parts = [product(columns[earlier].T, factor_rows) for earlier in range(later)]
        window_parts.append(product(factor_rows.T, current))
        window_sums = lax.psum(jnp.stack(window_parts), ("prow", "pcol"))
        window_step(later, window_sums, window_factor, diag_inverse, window_blocks)
        columns.append(current)
    ys = jnp.stack(columns).reshape(supernodes, tile_rows, 1, slice_rows, width)
    whole_window = assemble_window(window_blocks, supernodes)
    rows_each = supernodes * width // prow_count
    cols_each = supernodes * width // pcol_count
    local_window = lax.dynamic_slice(
        whole_window, (row_index * rows_each, column_index * cols_each), (rows_each, cols_each)
    )
    return (ys, local_window)


def solution(mesh):
    placed = (
        P(None, "prow", None, None, "pcol", None),
        P(None, None, "prow", "pcol", None),
        P(),
        P(),
        P(),
    )
    return jax.shard_map(
        per_device,
        mesh=mesh,
        in_specs=placed,
        out_specs=(P(None, None, "prow", "pcol", None), P("prow", "pcol")),
        check_vma=False,
    )
```

profile of v0, /device:TPU:4, one launch (start us, length us, event | category | flops | bytes accessed | tf_op | source)
XLA Modules:
  0.0 1206.1 jit_solution(4849116906709062268)
XLA Ops:
  9.8 70.2 %all_gather.12 = bf16[2,256,256]{2,0,1:T(2,128)(2,1)S(1)} all-gather(bf16[2,8,256]{2,0,1:T(2,128)(2,1)S(1)} %copy.58), channel_id=1, replica_groups=mesh['prow'=16,'pcol'=32] {'pcol'}, dimensions={1}, use_global_device_ids=true | all-gather | bytes 270336 | tf_op jit(solution)/shard_map/all_gather | solution.py:75
  80.4 59.8 %all_gather.13 = bf16[2,256,256]{2,0,1:T(2,128)(2,1)S(1)} all-gather(bf16[2,8,256]{2,0,1:T(2,128)(2,1)S(1)} %copy.63), channel_id=1, replica_groups=mesh['prow'=16,'pcol'=32] {'pcol'}, dimensions={1}, use_global_device_ids=true | all-gather | bytes 270336 | tf_op jit(solution)/shard_map/all_gather | solution.py:75
  142.0 61.7 %all_gather.15 = bf16[2,256,256]{2,0,1:T(2,128)(2,1)S(1)} all-gather(bf16[2,8,256]{2,0,1:T(2,128)(2,1)S(1)} %copy.73), channel_id=1, replica_groups=mesh['prow'=16,'pcol'=32] {'pcol'}, dimensions={1}, use_global_device_ids=true | all-gather | bytes 270336 | tf_op jit(solution)/shard_map/all_gather | solution.py:75
  204.8 59.8 %all_gather.14 = bf16[2,256,256]{2,0,1:T(2,128)(2,1)S(1)} all-gather(bf16[2,8,256]{2,0,1:T(2,128)(2,1)S(1)} %copy.68), channel_id=1, replica_groups=mesh['prow'=16,'pcol'=32] {'pcol'}, dimensions={1}, use_global_device_ids=true | all-gather | bytes 270336 | tf_op jit(solution)/shard_map/all_gather | solution.py:75
  265.8 141.1 %all-reduce.15.cloned.1.call-done = (bf16[256,256]{0,1:T(8,128)(2,1)}, bf16[256,256]{0,1:T(8,128)(2,1)}, bf16[256,256]{0,1:T(8,128)(2,1)}, bf16[256,256]{0,1:T(8,128)(2,1)}) async-done(((bf16[256,256]{0,1:T(8,128)(2,1)}, bf16[256,256]{0,1:T(8,128)(2,1)}, bf16[256,256]{0,1:T(8,128)(2,1)}, bf16[256,256]{0,1:T(8,128)(2,1)}), (bf16[256,256]{0,1:T(8,128)(2,1)}, bf16[256,256]{0,1:T(8,128)(2,1)}, ...) | async-done | bytes 524304 | tf_op jit(solution)/shard_map/psum | solution.py:9
  406.9 1.2 convolution_bitcast_fusion
  408.1 1.0 copy.75
  409.3 1.0 copy.60
  410.6 1.0 copy.65
  411.9 1.0 copy.70
  416.5 5.0 broadcast_select_fusion
  421.6 1.3 dynamic-slice.31
  423.5 262.1 %all-reduce.13.cloned.1.call-done = (f32[256,2,256]{2,1,0:T(2,128)}, f32[256,2,256]{2,1,0:T(2,128)}, f32[256,2,256]{2,1,0:T(2,128)}, f32[256,2,256]{2,1,0:T(2,128)}) async-done(((f32[256,2,256]{2,1,0:T(2,128)}, f32[256,2,256]{2,1,0:T(2,128)}, f32[256,2,256]{2,1,0:T(2,128)}, f32[256,2,256]{2,1,0:T(2,128)}), (f32[256,2,256]{2,1,0:T(2,128)}, f32[256,2,256]{2,1,0:T(2,128)}, f32[256,2,256]{2,1,0:T(2,128)}, ...) | async-done | bytes 2097168
  687.6 1.1 convolution_bitcast_fusion.19
  695.0 0.9 pad_maximum_fusion.1
  696.0 1.1 pad_maximum_fusion
  697.8 481.1 %all-reduce.11.cloned.1.call-done = (f32[1,256,256]{2,1,0:T(8,128)}, f32[4,256,256]{2,1,0:T(8,128)}, f32[2,256,256]{2,1,0:T(8,128)}, f32[3,256,256]{2,1,0:T(8,128)}) async-done(((f32[1,256,256]{2,1,0:T(8,128)}, f32[4,256,256]{2,1,0:T(8,128)}, f32[2,256,256]{2,1,0:T(8,128)}, f32[3,256,256]{2,1,0:T(8,128)}), (f32[1,256,256]{2,1,0:T(8,128)}, f32[4,256,256]{2,1,0:T(8,128)}, f32[2,256,256]{2,1,0:T(8,128)}, ...) | async-done | bytes 2621456 | tf_op jit(solution)/shard_map/psum | solution.py:106
  1178.9 1.0 subtract_bitcast_fusion
  1179.9 1.3 fusion.14
  1183.6 1.0 fusion.7
  1189.4 1.2 fusion.6
  1191.4 2.0 fusion.3
  1195.8 1.9 fusion.1
  1197.9 1.1 maximum_maximum_fusion
  (116 shorter events, 31.3 us)
Async XLA Ops:
  7.2 399.7 %copy-start = (bf16[2,1,256,1,1,256]{5,2,4,3,1,0:T(8,128)(2,1)S(1)}, bf16[2,1,256,1,1,256]{5,2,4,3,1,0:T(8,128)(2,1)}, u32[]{:S(2)}) copy-start(bf16[2,1,256,1,1,256]{5,2,4,3,1,0:T(8,128)(2,1)} %param.15) | copy-start | bytes 786436
  7.2 399.7 %all-reduce.15.cloned.1.call-start = ((), (), s32[]{:S(2)}) async-start(), calls=%async_computation.2 | async-start | bytes 1048576 | tf_op jit(solution)/shard_map/psum | solution.py:9
  265.7 420.0 %all-reduce.13.cloned.1.call-start = ((), (), s32[]{:S(2)}) async-start(), calls=%async_computation.1 | async-start | bytes 4194304
  406.9 2.2 copy-start.11
  409.1 1.3 copy-start.10
  410.3 1.3 copy-start.9
  412.9 3.6 copy-start.12
  412.9 273.5 %copy-start.8 = (bf16[4,2,1,8,256]{4,3,2,1,0:T(8,128)(2,1)S(1)}, bf16[4,2,1,8,256]{4,3,2,1,0:T(8,128)(2,1)}, u32[]{:S(2)}) copy-start(bf16[4,2,1,8,256]{4,3,2,1,0:T(8,128)(2,1)} %param.16) | copy-start | bytes 98308
  412.9 277.2 %copy-start.1 = (bf16[6,256,256]{2,1,0:T(8,128)(2,1)S(1)}, bf16[6,256,256]{2,1,0:T(8,128)(2,1)}, u32[]{:S(2)}) copy-start(bf16[6,256,256]{2,1,0:T(8,128)(2,1)} %param.18) | copy-start | bytes 2359300
  412.9 765.9 %all-reduce.11.cloned.1.call-start = ((), (), s32[]{:S(2)}) async-start(), calls=%async_computation | async-start | bytes 5242880 | tf_op jit(solution)/shard_map/psum | solution.py:106
  697.1 481.8 %copy-start.7 = (bf16[4,256,256]{2,1,0:T(8,128)(2,1)S(1)}, bf16[4,256,256]{2,1,0:T(8,128)(2,1)}, u32[]{:S(2)}) copy-start(bf16[4,256,256]{2,1,0:T(8,128)(2,1)} %param.19) | copy-start | bytes 1572868
  1178.9 2.4 copy-start.6
  1179.9 1.7 copy-start.2
  1181.6 1.1 copy-start.5
  1188.4 0.9 copy-start.4
  1194.3 0.9 copy-start.3
Sparse Core Ops, SparseCore 0:
  265.8 140.9 all-reduce.14
  413.1 272.5 all-reduce.12
  697.2 481.5 all-reduce.10
where the time goes:
time: 1210 us
  waiting for transfers between devices  884 us (73%)
  blocking collectives  252 us (21%)
  local copies, waits for them, and re-layouts  20.5 us (2%)
  matrix products  19.6 us (2%)
  other arithmetic  15 us (1%)
  between operations  14.9 us (1%)
    psum x1, waiting for transfers between devices, per_device(): window_sums = lax.psum(jnp.stack(window_parts), ('prow', 'pcol'))  481 us
    unnamed x4, waiting for transfers between devices  262 us
    all_gather x4, blocking collectives, per_device(): full_rows = lax.all_gather(own_piece, 'pcol', axis=1, tiled=True)  252 us
    psum x1, waiting for transfers between devices, broadcast(): return lax.psum(block, axis)  141 us
  transfers between devices with their start and end apart: 3, of which 3 were waited for; matrix products, arithmetic and copies ran while one was open for 1% of the time, Pallas kernels for 0%

commit v1 on v0

--- a/solution.py
+++ b/solution.py
@@ -103,7 +103,7 @@
         factor_rows = own_piece.reshape(tile_rows * slice_rows, width).astype(jnp.float32)
         window_parts = [product(columns[earlier].T, factor_rows) for earlier in range(later)]
         window_parts.append(product(factor_rows.T, current))
-        window_sums = lax.psum(jnp.stack(window_parts), ("prow", "pcol"))
+        window_sums = lax.psum(lax.psum(jnp.stack(window_parts), "pcol"), "prow")
         window_step(later, window_sums, window_factor, diag_inverse, window_blocks)
         columns.append(current)
     ys = jnp.stack(columns).reshape(supernodes, tile_rows, 1, slice_rows, width)

time: 1210 us -> 1140 us (0.942)
  the two profiles are of different devices: /device:TPU:4 before, /device:TPU:7 now
where the time goes in v1:
time: 1140 us
  waiting for transfers between devices  875 us (77%)
  blocking collectives  197 us (17%)
  local copies, waits for them, and re-layouts  20.5 us (2%)
  matrix products  19.6 us (2%)
  other arithmetic  15 us (1%)
  between operations  14.9 us (1%)
    psum x2, waiting for transfers between devices, per_device(): window_sums = lax.psum(lax.psum(jnp.stack(window_parts), 'pcol'), 'prow')  439 us
    unnamed x5, waiting for transfers between devices  233 us
    psum x1, waiting for transfers between devices, broadcast(): return lax.psum(block, axis)  203 us
    all_gather x4, blocking collectives, per_device(): full_rows = lax.all_gather(own_piece, 'pcol', axis=1, tiled=True)  197 us
  transfers between devices with their start and end apart: 4, of which 4 were waited for; matrix products, arithmetic and copies ran while one was open for 1% of the time, Pallas kernels for 0%

profile of v1, /device:TPU:7, one launch (start us, length us, event | category | flops | bytes accessed | tf_op | source)
XLA Modules:
  0.0 1141.5 jit_solution(18065701218539782110)
XLA Ops:
  9.8 56.2 %all_gather.12 = bf16[2,256,256]{2,0,1:T(2,128)(2,1)S(1)} all-gather(bf16[2,8,256]{2,0,1:T(2,128)(2,1)S(1)} %copy.58), channel_id=1, replica_groups=mesh['prow'=16,'pcol'=32] {'pcol'}, dimensions={1}, use_global_device_ids=true | all-gather | bytes 270336 | tf_op jit(solution)/shard_map/all_gather | solution.py:75
  66.4 46.0 %all_gather.13 = bf16[2,256,256]{2,0,1:T(2,128)(2,1)S(1)} all-gather(bf16[2,8,256]{2,0,1:T(2,128)(2,1)S(1)} %copy.63), channel_id=1, replica_groups=mesh['prow'=16,'pcol'=32] {'pcol'}, dimensions={1}, use_global_device_ids=true | all-gather | bytes 270336 | tf_op jit(solution)/shard_map/all_gather | solution.py:75
  114.2 48.3 %all_gather.15 = bf16[2,256,256]{2,0,1:T(2,128)(2,1)S(1)} all-gather(bf16[2,8,256]{2,0,1:T(2,128)(2,1)S(1)} %copy.73), channel_id=1, replica_groups=mesh['prow'=16,'pcol'=32] {'pcol'}, dimensions={1}, use_global_device_ids=true | all-gather | bytes 270336 | tf_op jit(solution)/shard_map/all_gather | solution.py:75
  163.6 46.0 %all_gather.14 = bf16[2,256,256]{2,0,1:T(2,128)(2,1)S(1)} all-gather(bf16[2,8,256]{2,0,1:T(2,128)(2,1)S(1)} %copy.68), channel_id=1, replica_groups=mesh['prow'=16,'pcol'=32] {'pcol'}, dimensions={1}, use_global_device_ids=true | all-gather | bytes 270336 | tf_op jit(solution)/shard_map/all_gather | solution.py:75
  210.8 203.1 %all-reduce.19.cloned.1.call-done = (bf16[256,256]{0,1:T(8,128)(2,1)}, bf16[256,256]{0,1:T(8,128)(2,1)}, bf16[256,256]{0,1:T(8,128)(2,1)}, bf16[256,256]{0,1:T(8,128)(2,1)}) async-done(((bf16[256,256]{0,1:T(8,128)(2,1)}, bf16[256,256]{0,1:T(8,128)(2,1)}, bf16[256,256]{0,1:T(8,128)(2,1)}, bf16[256,256]{0,1:T(8,128)(2,1)}), (bf16[256,256]{0,1:T(8,128)(2,1)}, bf16[256,256]{0,1:T(8,128)(2,1)}, ...) | async-done | bytes 524304 | tf_op jit(solution)/shard_map/psum | solution.py:9
  413.9 1.2 convolution_bitcast_fusion
  415.1 1.0 copy.75
  416.4 1.0 copy.60
  417.7 1.0 copy.65
  419.0 1.0 copy.70
  423.4 5.0 broadcast_select_fusion
  428.5 1.3 dynamic-slice.31
  430.4 232.5 %all-reduce.15.cloned.1.call-done = (f32[256,2,256]{2,1,0:T(2,128)}, f32[256,2,256]{2,1,0:T(2,128)}, f32[256,2,256]{2,1,0:T(2,128)}, f32[256,2,256]{2,1,0:T(2,128)}) async-done(((f32[256,2,256]{2,1,0:T(2,128)}, f32[256,2,256]{2,1,0:T(2,128)}, f32[256,2,256]{2,1,0:T(2,128)}, f32[256,2,256]{2,1,0:T(2,128)}), (f32[256,2,256]{2,1,0:T(2,128)}, f32[256,2,256]{2,1,0:T(2,128)}, f32[256,2,256]{2,1,0:T(2,128)}, ...) | async-done | bytes 2097168
  664.8 1.1 convolution_bitcast_fusion.19
  673.3 1.1 pad_maximum_fusion
  674.6 259.3 %all-reduce.13.cloned.1.call-done = (f32[1,256,256]{2,1,0:T(8,128)}, f32[4,256,256]{2,1,0:T(8,128)}, f32[2,256,256]{2,1,0:T(8,128)}, f32[3,256,256]{2,1,0:T(8,128)}) async-done(((f32[1,256,256]{2,1,0:T(8,128)}, f32[4,256,256]{2,1,0:T(8,128)}, f32[2,256,256]{2,1,0:T(8,128)}, f32[3,256,256]{2,1,0:T(8,128)}), (f32[1,256,256]{2,1,0:T(8,128)}, f32[4,256,256]{2,1,0:T(8,128)}, f32[2,256,256]{2,1,0:T(8,128)}, ...) | async-done | bytes 2621456 | tf_op jit(solution)/shard_map/psum | solution.py:106
  934.6 179.6 %all-reduce.17.cloned.1.call-done = (f32[1,256,256]{2,1,0:T(8,128)}, f32[4,256,256]{2,1,0:T(8,128)}, f32[2,256,256]{2,1,0:T(8,128)}, f32[3,256,256]{2,1,0:T(8,128)}) async-done(((f32[1,256,256]{2,1,0:T(8,128)}, f32[4,256,256]{2,1,0:T(8,128)}, f32[2,256,256]{2,1,0:T(8,128)}, f32[3,256,256]{2,1,0:T(8,128)}), (f32[1,256,256]{2,1,0:T(8,128)}, f32[4,256,256]{2,1,0:T(8,128)}, f32[2,256,256]{2,1,0:T(8,128)}, ...) | async-done | bytes 2621456 | tf_op jit(solution)/shard_map/psum | solution.py:106
  1114.2 1.0 subtract_bitcast_fusion
  1115.3 1.3 fusion.14
  1119.0 1.0 fusion.7
  1124.7 1.2 fusion.6
  1126.8 2.0 fusion.3
  1131.2 1.9 fusion.1
  1133.2 1.1 maximum_maximum_fusion
  (119 shorter events, 32.3 us)
Async XLA Ops:
  7.2 406.8 %copy-start = (bf16[2,1,256,1,1,256]{5,2,4,3,1,0:T(8,128)(2,1)S(1)}, bf16[2,1,256,1,1,256]{5,2,4,3,1,0:T(8,128)(2,1)}, u32[]{:S(2)}) copy-start(bf16[2,1,256,1,1,256]{5,2,4,3,1,0:T(8,128)(2,1)} %param.15) | copy-start | bytes 786436
  7.2 406.8 %all-reduce.19.cloned.1.call-start = ((), (), s32[]{:S(2)}) async-start(), calls=%async_computation.3 | async-start | bytes 1048576 | tf_op jit(solution)/shard_map/psum | solution.py:9
  210.8 452.2 %all-reduce.15.cloned.1.call-start = ((), (), s32[]{:S(2)}) async-start(), calls=%async_computation.1 | async-start | bytes 4194304
  413.9 2.2 copy-start.11
  416.1 1.3 copy-start.10
  417.4 1.3 copy-start.9
  420.0 3.4 copy-start.12
  420.0 243.7 %copy-start.8 = (bf16[4,2,1,8,256]{4,3,2,1,0:T(8,128)(2,1)S(1)}, bf16[4,2,1,8,256]{4,3,2,1,0:T(8,128)(2,1)}, u32[]{:S(2)}) copy-start(bf16[4,2,1,8,256]{4,3,2,1,0:T(8,128)(2,1)} %param.16) | copy-start | bytes 98308
  420.0 247.4 %copy-start.1 = (bf16[6,256,256]{2,1,0:T(8,128)(2,1)S(1)}, bf16[6,256,256]{2,1,0:T(8,128)(2,1)}, u32[]{:S(2)}) copy-start(bf16[6,256,256]{2,1,0:T(8,128)(2,1)} %param.18) | copy-start | bytes 2359300
  420.0 513.8 %all-reduce.13.cloned.1.call-start = ((), (), s32[]{:S(2)}) async-start(), calls=%async_computation | async-start | bytes 5242880 | tf_op jit(solution)/shard_map/psum | solution.py:106
  674.3 439.9 %all-reduce.17.cloned.1.call-start = ((), (), s32[]{:S(2)}) async-start(), calls=%async_computation.2 | async-start | bytes 5242880 | tf_op jit(solution)/shard_map/psum | solution.py:106
  933.9 180.3 %copy-start.7 = (bf16[4,256,256]{2,1,0:T(8,128)(2,1)S(1)}, bf16[4,256,256]{2,1,0:T(8,128)(2,1)}, u32[]{:S(2)}) copy-start(bf16[4,256,256]{2,1,0:T(8,128)(2,1)} %param.19) | copy-start | bytes 1572868
  1114.2 2.4 copy-start.6
  1115.3 1.7 copy-start.2
  1116.9 1.1 copy-start.5
  1123.8 0.9 copy-start.4
  1129.6 0.9 copy-start.3
Sparse Core Ops, SparseCore 0:
  210.9 203.0 all-reduce.18
  420.1 242.7 all-reduce.14
  674.5 259.3 all-reduce.12
  936.9 177.2 all-reduce.16
